TPU v7x, 32 devices: a whole 2x2x4 slice. The times are simulated.
32 devices in a mesh: ctx: 8 (over z, x), ch: 4 (over y, core).
Axes of the slice: x: 2, y: 2, z: 4, core: 2. Of those that a mesh axis runs over, the one named last changes fastest.
Arguments:
- signal: float32 [64, 65536], P('ch', 'ctx'), parts along dimension 0, may hold values from -6 to 6
- gate: float32 [64, 65536], P('ch', 'ctx'), parts along dimension 0, may hold values from -6 to 6
- skip: float32 [64], P('ch'), parts along dimension 0, may hold values from 0.5 to 1.5
- filter_spectrum: float32 [16, 2, 64, 8192], P('ctx', None, 'ch'), parts along dimension 2, may hold values from -6 to 6
Outputs:
- gated: float32 [64, 65536], P('ch', 'ctx'), parts along dimension 0
There are 4 independent parts, one for each index of `ch`. A program takes and returns all parts, laid end to end along the dimension named above; each array names one. Nothing has to cross between parts.
All inputs are finite; a program needn't handle non-finite values.
Results may differ from a plain program's by a relative error of at most 0.00005.
Values sent between devices are 32-bit elements; how exact they have to be, the bound alone decides.
No kernel may reach another device: no remote copies, remote signals or barrier semaphores. Data moves between devices by JAX's collectives and lax.ppermute only.
A program may use at most 128 MiB of HBM per device.

v0:
```python
import math

import jax
import jax.numpy as jnp
from jax import lax
from jax.sharding import PartitionSpec as P


def contract(form, left, right):
    return jnp.einsum(form, left, right, precision=lax.Precision.HIGHEST)


def phase_table(left, right, period):
    angle = left * right % period
    theta = angle.astype(jnp.float32) * (2.0 * math.pi / period)
    return (jnp.cos(theta), jnp.sin(theta))


def product_pair(form, left, right):
    real_part = contract(form, left[0], right[0]) - contract(form, left[1], right[1])
    imag_part = contract(form, left[0], right[1]) + contract(form, left[1], right[0])
    return (real_part, imag_part)


def times_pair(left, right):
    return (left[0] * right[0] - left[1] * right[1], left[0] * right[1] + left[1] * right[0])


def local_tables(length):
    outer_len = 128
    inner_len = length // outer_len
    outer_index = jnp.arange(outer_len, dtype=jnp.int32)
    inner_index = jnp.arange(inner_len, dtype=jnp.int32)
    outer_wave = phase_table(outer_index[:, None], outer_index[None, :], outer_len)
    twist_wave = phase_table(outer_index[:, None], inner_index[None, :], length)
    inner_wave = phase_table(inner_index[:, None], inner_index[None, :], inner_len)
    return (outer_len, inner_len, outer_wave, twist_wave, inner_wave)


def local_forward(values, length):
    outer_len, inner_len, outer_wave, twist_wave, inner_wave = local_tables(length)
    lead_shape = values[0].shape[:-1]
    values = tuple((part.reshape(lead_shape + (outer_len, inner_len)) for part in values))
    values = product_pair("as,...sb->...ab", (outer_wave[0], -outer_wave[1]), values)
    values = times_pair(values, (twist_wave[0], -twist_wave[1]))
    return product_pair("...as,bs->...ab", values, (inner_wave[0], -inner_wave[1]))


def local_inverse(values, length):
    outer_len, inner_len, outer_wave, twist_wave, inner_wave = local_tables(length)
    lead_shape = values[0].shape[:-2]
    values = product_pair("...ak,sk->...as", values, inner_wave)
    values = times_pair(values, twist_wave)
    values = product_pair("ta,...as->...ts", outer_wave, values)
    return tuple((part.reshape(lead_shape + (length,)) for part in values))


def shards(signal, gate, skip, filter_spectrum):
    parts_count = lax.axis_size("ctx")
    freq_rows = 2 * parts_count
    channels, tok_local = signal.shape
    slice_len = tok_local // parts_count
    full_len = freq_rows * tok_local
    device = lax.axis_index("ctx")
    is_first = device == 0
    columns = lax.all_to_all(signal[None], "ctx", split_axis=2, concat_axis=0, tiled=True)
    source_row = jnp.arange(parts_count, dtype=jnp.int32)
    dest_index = jnp.arange(parts_count, dtype=jnp.int32)
    slice_pos = device * slice_len + jnp.arange(slice_len, dtype=jnp.int32)
    upper_freq = jnp.where(dest_index == 0, parts_count, freq_rows - dest_index)
    row_freq = jnp.stack([dest_index, upper_freq], axis=1).reshape(freq_rows)
    spot = jnp.arange(tok_local, dtype=jnp.int32)
    wave_cos, wave_sin = phase_table(row_freq[:, None], source_row[None, :], freq_rows)
    first_re = contract("kr,rcq->kcq", wave_cos, columns)
    first_im = -contract("kr,rcq->kcq", wave_sin, columns)
    twist_cos, twist_sin = phase_table(row_freq[:, None], slice_pos[None, :], full_len)
    first_pair = times_pair((first_re, first_im), (twist_cos[:, None, :], -twist_sin[:, None, :]))
    stacked = jnp.stack(first_pair, axis=1)
    moved = lax.all_to_all(stacked, "ctx", split_axis=0, concat_axis=3, tiled=True)
    low_pair = (moved[0, 0], moved[0, 1])
    high_pair = (moved[1, 0], moved[1, 1])
    rows_pair = (jnp.stack([low_pair[0], high_pair[0]]), jnp.stack([low_pair[1], high_pair[1]]))
    spectral = local_forward(rows_pair, tok_local)
    inner_len = tok_local // 128
    filt = filter_spectrum.reshape(2, 2, channels, inner_len, 128).swapaxes(3, 4)
    product = times_pair(spectral, (filt[:, 0], filt[:, 1]))
    restored = local_inverse(product, tok_local)
    my_freq = jnp.stack([device, jnp.where(is_first, parts_count, freq_rows - device)])
    back_cos, back_sin = phase_table(my_freq[:, None], spot[None, :], full_len)
    turned = times_pair(restored, (back_cos[:, None, :], back_sin[:, None, :]))
    scale_factor = 1.0 / full_len
    stacked = jnp.stack(turned, axis=1)
    moved = lax.all_to_all(stacked, "ctx", split_axis=3, concat_axis=0, tiled=True)
    out_cos, out_sin = phase_table(source_row[:, None], row_freq[None, :], freq_rows)
    rows_all = contract("rm,mcq->rcq", out_cos, moved[:, 0]) - contract(
        "rm,mcq->rcq", out_sin, moved[:, 1]
    )
    rows_all = rows_all * scale_factor
    convolved = lax.all_to_all(rows_all, "ctx", split_axis=0, concat_axis=2, tiled=True)
    return gate * (convolved[0] + skip[:, None] * signal)


def solution(mesh):
    return jax.shard_map(
        shards,
        mesh=mesh,
        in_specs=(P("ch", "ctx"), P("ch", "ctx"), P("ch"), P("ctx", None, "ch", None)),
        out_specs=P("ch", "ctx"),
        check_vma=False,
    )
```

profile of v0, /device:TPU:0, one launch (start us, length us, event | category | flops | bytes accessed | tf_op | source)
XLA Modules:
  0.0 350.9 jit_solution(4517637440117171831)
XLA Ops:
  0.0 3.5 copy.33
  4.0 38.3 %reduce = f32[8192,16]{1,0:T(8,128)} reduce(f32[8192,1,16]{2,1,0:T(1,128)} %bitcast.158, f32[]{:T(128)} %broadcast.483), dimensions={1}, to_apply=%bitcast.139.reduce_sub_computation | reduce | bytes 1048580
  42.3 4.4 %reshape.260 = f32[8,1,16384]{2,1,0:T(1,128)} reshape(f32[8192,16]{1,0:T(8,128)} %reduce) | data formatting | bytes 1048576
  46.7 7.5 %all-to-all-start = ((f32[8,1,16384]{2,1,0:T(1,128)}), f32[8,1,16384]{2,1,0:T(1,128)S(1)}, u32[]{:S(2)}, u32[]{:S(2)}) async-start(f32[8,1,16384]{2,1,0:T(1,128)} %reshape.260), calls=%async_computation | async-start | bytes 1048576 | tf_op jit(solution)/shard_map/all_to_all | solution.py:66
  54.8 13.9 %all-to-all-done = f32[8,1,16384]{2,1,0:T(1,128)S(1)} async-done(((f32[8,1,16384]{2,1,0:T(1,128)}), f32[8,1,16384]{2,1,0:T(1,128)S(1)}, u32[]{:S(2)}, u32[]{:S(2)}) %all-to-all-start) | async-done | bytes 524320 | tf_op jit(solution)/shard_map/all_to_all | solution.py:66
  68.7 1.8 reduce.1
  70.5 10.2 %reshape.261 = f32[8192,1,16]{2,1,0:T(1,128)} reshape(f32[8,16384]{1,0:T(8,128)S(1)} %reduce.1) | data formatting | bytes 1048576
  80.7 2.9 copy.55
  86.2 2.5 copy.35
  88.7 3.6 %all-to-all-start.1 = ((f32[16,2,16,1024]{3,2,1,0:T(8,128)}), f32[16,2,16,1024]{3,2,1,0:T(8,128)S(1)}, u32[]{:S(2)}, u32[]{:S(2)}) async-start(f32[16,2,16,1024]{3,2,1,0:T(8,128)} %copy.35), calls=%async_computation.1 | async-start | bytes 4194304 | tf_op jit(solution)/shard_map/all_to_all | solution.py:79
  92.3 2.0 copy.58
  94.3 1.5 copy.63
  97.4 43.4 %all-to-all-done.1 = f32[16,2,16,1024]{3,2,1,0:T(8,128)S(1)} async-done(((f32[16,2,16,1024]{3,2,1,0:T(8,128)}), f32[16,2,16,1024]{3,2,1,0:T(8,128)S(1)}, u32[]{:S(2)}, u32[]{:S(2)}) %all-to-all-start.1) | async-done | bytes 2097184 | tf_op jit(solution)/shard_map/all_to_all | solution.py:79
  140.8 2.5 copy.64
  143.3 2.2 all_to_all.57
  149.9 1.5 stack.47
  160.8 1.9 multiply_add_fusion.2
  168.7 2.2 fusion.13
  172.1 2.0 copy.43
  174.1 2.1 reshape.248
  176.2 3.5 fusion.1
  179.7 1.8 copy.42
  181.5 1.6 reshape.247
  184.7 15.4 %copy.44 = f32[2,2,16,8192]{2,0,1,3:T(2,128)} copy(f32[2,2,16,8192]{3,2,0,1:T(8,128)S(1)} %pad_maximum_fusion.1) | data formatting | bytes 4194304 | tf_op jit(solution)/shard_map/stack | solution.py:92
  200.1 24.0 %reshape.262 = f32[8,1,65536]{2,1,0:T(1,128)S(1)} reshape(f32[8192,2,2,16]{3,2,1,0:T(2,128)} %bitcast.155) | data formatting | bytes 4194304
  224.2 51.9 %all_to_all.69 = f32[8,1,65536]{2,1,0:T(1,128)} all-to-all(f32[8,1,65536]{2,1,0:T(1,128)S(1)} %reshape.262), channel_id=1, replica_groups=mesh['ctx'=8,'ch'=4] {'ctx'}, dimensions={0} | all-to-all | bytes 4194304 | tf_op jit(solution)/shard_map/all_to_all | solution.py:93
  276.1 7.1 %reduce.2 = f32[8,65536]{1,0:T(8,128)S(1)} reduce(f32[8,1,65536]{2,1,0:T(1,128)} %all_to_all.69, f32[]{:T(128)} %broadcast.483), dimensions={1}, to_apply=%all_to_all.58.reduce_sub_computation | reduce | bytes 4194308 | tf_op jit(solution)/shard_map/all_to_all | solution.py:93
  283.2 28.4 %reshape.263 = f32[8192,2,2,16]{3,2,1,0:T(2,128)} reshape(f32[8,65536]{1,0:T(8,128)S(1)} %reduce.2) | data formatting | bytes 4194304
  311.6 13.2 %copy.57 = f32[2,2,16,8,1024]{4,3,2,1,0:T(8,128)S(1)} copy(f32[2,2,16,8,1024]{2,0,1,4,3:T(2,128)} %bitcast.156) | data formatting | bytes 4194304 | tf_op jit(solution)/shard_map/all_to_all | solution.py:93
  324.9 3.0 copy.46
  327.8 2.7 all_to_all.61
  332.2 17.6 %all_to_all.70 = f32[8,16,1024]{2,1,0:T(8,128)S(1)} all-to-all(f32[8,16,1024]{2,1,0:T(8,128)S(1)} %copy.47), channel_id=1, replica_groups=mesh['ctx'=8,'ch'=4] {'ctx'}, dimensions={0} | all-to-all | bytes 1048576 | tf_op jit(solution)/shard_map/all_to_all | solution.py:99
  (51 shorter events, 30.3 us)
Async XLA Ops:
  46.7 21.9 %all-to-all-start = ((f32[8,1,16384]{2,1,0:T(1,128)}), f32[8,1,16384]{2,1,0:T(1,128)S(1)}, u32[]{:S(2)}, u32[]{:S(2)}) async-start(f32[8,1,16384]{2,1,0:T(1,128)} %reshape.260), calls=%async_computation | async-start | bytes 1048576 | tf_op jit(solution)/shard_map/all_to_all | solution.py:66
  88.7 52.1 %all-to-all-start.1 = ((f32[16,2,16,1024]{3,2,1,0:T(8,128)}), f32[16,2,16,1024]{3,2,1,0:T(8,128)S(1)}, u32[]{:S(2)}, u32[]{:S(2)}) async-start(f32[16,2,16,1024]{3,2,1,0:T(8,128)} %copy.35), calls=%async_computation.1 | async-start | bytes 4194304 | tf_op jit(solution)/shard_map/all_to_all | solution.py:79
  159.3 1.6 copy-start
  331.8 18.0 %copy-start.1 = (f32[16,8192]{1,0:T(8,128)S(1)}, f32[16,8192]{1,0:T(8,128)}, u32[]{:S(2)}) copy-start(f32[16,8192]{1,0:T(8,128)} %param.4) | copy-start | bytes 1572868
  331.9 18.0 %copy-start.2 = (f32[16,8192]{1,0:T(8,128)S(1)}, f32[16,8192]{1,0:T(8,128)}, u32[]{:S(2)}) copy-start(f32[16,8192]{1,0:T(8,128)} %param.5) | copy-start | bytes 1572868
  331.9 18.0 %copy-start.3 = (f32[16]{0:T(128)S(1)}, f32[16]{0:T(128)}, u32[]{:S(2)}) copy-start(f32[16]{0:T(128)} %param.6) | copy-start | bytes 196
where the time goes:
time: 357 us; the launch traced here: 351 us
  local copies, waits for them, and re-layouts  133 us (37%)
  blocking collectives  69.5 us (19%)
  waiting for transfers between devices  57.2 us (16%)
  other arithmetic  52 us (15%)
  matrix products  27.2 us (8%)
  starting transfers between devices  11.1 us (3%)
    unnamed x16, local copies, waits for them, and re-layouts  73.3 us
    all_to_all x1, blocking collectives, shards(): lax.all_to_all(stacked, 'ctx', split_axis=3, concat_axis=0, tiled=True)  51.9 us
    all_to_all x1, waiting for transfers between devices, shards(): lax.all_to_all(stacked, 'ctx', split_axis=0, concat_axis=3, tiled=True)  43.4 us
    unnamed x1, other arithmetic  38.3 us
    dot_general x20, matrix products, contract(): return jnp.einsum(form, left, right, precision=lax.Precision.HIGHEST)  27.2 us
    all_to_all x3, local copies, waits for them, and re-layouts, shards(): lax.all_to_all(stacked, 'ctx', split_axis=3, concat_axis=0, tiled=True)  18.9 us
    all_to_all x1, blocking collectives, shards(): lax.all_to_all(rows_all, 'ctx', split_axis=0, concat_axis=2, tiled=True)  17.6 us
    another operation x1, local copies, waits for them, and re-layouts, shards(): stacked = jnp.stack(turned, axis=1)  15.4 us
  transfers between devices with their start and end apart: 2, of which 2 were waited for; matrix products, arithmetic and copies ran while one was open for 2% of the time, Pallas kernels for 0%

commit v1 on v0

--- a/solution.py
+++ b/solution.py
@@ -1,9 +1,269 @@
+import functools
 import math
 
 import jax
 import jax.numpy as jnp
+import numpy as np
 from jax import lax
+from jax.experimental import pallas as pl
+from jax.experimental.pallas import tpu as pltpu
 from jax.sharding import PartitionSpec as P
+
+LANES = 128
+HALF = LANES // 2
+
+
+def split_pair(values):
+    high = values.astype(jnp.bfloat16)
+    low = (values - high.astype(jnp.float32)).astype(jnp.bfloat16)
+    return high, low
+
+
+def split_table(table):
+    table = np.asarray(table, np.float32)
+    high = table.astype(jnp.bfloat16)
+    low = (table - high.astype(np.float32)).astype(jnp.bfloat16)
+    return np.stack([high, low])
+
+
+def multiply(left, right, dims):
+    def dot(a, b):
+        return lax.dot_general(a, b, (dims, ((), ())), preferred_element_type=jnp.float32)
+
+    return dot(left[0], right[0]) + (dot(left[0], right[1]) + dot(left[1], right[0]))
+
+
+ROWS_COLS = ((1,), (0,))
+COLS_COLS = ((0,), (0,))
+
+
+@functools.lru_cache(maxsize=None)
+def tables(parts, blocks):
+    freq_rows = 2 * parts
+    period = freq_rows * blocks
+    full_len = period * LANES
+    rows = np.arange(parts * blocks)
+    index = np.zeros((parts, blocks), np.int64)
+    for owner in range(parts):
+        for place in range(blocks):
+            if owner:
+                index[owner, place] = freq_rows * place + owner
+            elif place < blocks // 2:
+                index[owner, place] = freq_rows * place
+            else:
+                index[owner, place] = freq_rows * (place - blocks // 2) + parts
+    index = index.reshape(-1)
+    angle = 2 * np.pi * ((index[:, None] * rows[None, :]) % period) / period
+    wave_re, wave_im = np.cos(angle), -np.sin(angle)
+    wave_im[0] = np.where(rows % 2 == 0, 1.0, -1.0)
+    outer = np.concatenate([wave_re, wave_im], axis=0)
+    lane = np.arange(LANES)
+    turn = 2 * np.pi * ((index[:, None] * lane[None, :]) % full_len) / full_len
+    twist = np.stack([np.cos(turn), np.sin(turn)])
+    twist[0, 0], twist[1, 0] = 1.0, 0.0
+    freq = 2 * (lane % HALF) + lane // HALF
+    theta = 2 * np.pi * ((lane[:, None] * freq[None, :]) % LANES) / LANES
+    cos, sin = np.cos(theta), np.sin(theta)
+    inner = np.block([[cos, -sin], [sin, cos]])
+    inner_back = np.block([[cos.T, sin.T], [-sin.T, cos.T]]) / full_len
+    upper = lane % HALF >= HALF // 2
+    half_theta = 2 * np.pi * ((lane[:, None] * (2 * freq[None, :] + 1)) % (2 * LANES)) / (2 * LANES)
+    alternate = np.where(lane % 2 == 0, 1.0, -1.0)
+    zero_re, zero_im = np.where(upper, 0.0, cos), np.where(upper, 0.0, -sin)
+    zero_re[:, 0], zero_im[:, 0] = 1.0, alternate
+    mid_re = np.where(upper, np.cos(half_theta), 0.0)
+    mid_im = np.where(upper, -np.sin(half_theta), 0.0)
+    edge = np.block([[zero_re, zero_im], [mid_re, mid_im]])
+    weight = np.ones(LANES)
+    weight[0] = 0.5
+    edge_back = np.block([[zero_re, mid_re], [zero_im, mid_im]])
+    back_re = np.concatenate([(zero_re * weight).T, mid_re.T], axis=1)
+    back_im = np.concatenate([(zero_im * weight).T, mid_im.T], axis=1)
+    edge_back = np.concatenate([back_re, back_im], axis=0) / full_len
+    return {
+        "outer": split_table(outer.T),
+        "twist": twist.astype(np.float32),
+        "inner": split_table(inner),
+        "edge": split_table(edge),
+        "inner_back": split_table(inner_back),
+        "edge_back": split_table(edge_back),
+    }
+
+
+def spread_kernel(signal_ref, out_ref):
+    channels, length = signal_ref.shape
+    blocks = length // LANES
+    for block in range(blocks):
+        out_ref[pl.ds(block, channels, stride=blocks), :] = signal_ref[:, block * LANES : (block + 1) * LANES]
+
+
+def fold_kernel(device_ref, filter_ref, out_ref, work_ref):
+    channels = filter_ref.shape[2]
+    blocks = filter_ref.shape[3] // LANES
+    lane = lax.broadcasted_iota(jnp.int32, (channels, LANES), 1)
+    reverse = LANES - 1 - lane
+    negate = (LANES - lane) % LANES
+
+    def tile(row, part, block):
+        return filter_ref[row, part, :, block * LANES : (block + 1) * LANES]
+
+    def pick(values, where):
+        return jnp.take_along_axis(values, where, axis=1)
+
+    def put(part, block, values):
+        work_ref[part, pl.ds(block, channels, stride=blocks), :] = values
+
+    @pl.when(device_ref[0] != 0)
+    def _():
+        for block in range(blocks):
+            mirror = blocks - 1 - block
+            put(0, block, tile(0, 0, block) + pick(tile(1, 0, mirror), reverse))
+            put(1, block, tile(0, 1, block) - pick(tile(1, 1, mirror), reverse))
+
+    @pl.when(device_ref[0] == 0)
+    def _():
+        place = lane % HALF
+        for block in range(blocks):
+            mirror, wrapped = blocks - 1 - block, (blocks - block) % blocks
+            for part in range(2):
+                sign = 1.0 - 2.0 * part
+                below = jnp.where(lane == 0, tile(0, part, wrapped), pick(tile(0, part, mirror), negate))
+                low = tile(0, part, block) + sign * below
+                high = tile(1, part, block) + sign * pick(tile(1, part, mirror), reverse)
+                values = jnp.where(place < HALF // 2, low, pltpu.roll(high, HALF // 2, 1))
+                if block >= blocks // 2:
+                    values = jnp.where(place == 0, pltpu.roll(low, LANES - HALF // 2, 1), values)
+                if block == 0 and part == 1:
+                    values = jnp.where(lane == 0, 2.0 * tile(0, 0, blocks // 2), values)
+                put(part, block, values)
+
+    left = lax.broadcasted_iota(jnp.int32, (blocks, LANES), 1) < HALF
+    for pair in range(channels // 2):
+        for part in range(2):
+            block = work_ref[part, pl.ds(pair * 2 * blocks, 2 * blocks), :]
+            turned = block.T
+            first, second = turned[:blocks], turned[blocks:]
+            out_ref[2 * pair, part] = jnp.where(left, first, pltpu.roll(second, HALF, 1))
+            out_ref[2 * pair + 1, part] = jnp.where(left, pltpu.roll(first, HALF, 1), second)
+
+
+def forward_kernel(x_ref, outer_ref, twist_ref, inner_ref, edge_ref, out_ref):
+    parts, own, blocks, _ = x_ref.shape
+    slots = parts * blocks
+    rows = jnp.concatenate(
+        [jnp.concatenate([x_ref[part, c] for part in range(parts)], axis=0) for c in range(own)], axis=1
+    )
+    first = multiply((outer_ref[0], outer_ref[1]), split_pair(rows), COLS_COLS)
+    cos, sin = twist_ref[0], twist_ref[1]
+    head = lax.broadcasted_iota(jnp.int32, (8, 2 * LANES), 0) == 0
+    for c in range(own):
+        re = first[:slots, c * LANES : (c + 1) * LANES]
+        im = first[slots:, c * LANES : (c + 1) * LANES]
+        turned = jnp.concatenate([re * cos + im * sin, im * cos - re * sin], axis=1)
+        pair = split_pair(turned)
+        spectrum = multiply(pair, (inner_ref[0], inner_ref[1]), ROWS_COLS)
+        edge = multiply((pair[0][:16], pair[1][:16]), (edge_ref[0], edge_ref[1]), ROWS_COLS)
+        out_ref[c, 0] = spectrum[:, :LANES]
+        out_ref[c, 1] = spectrum[:, LANES:]
+        top = jnp.where(head, edge[:8], spectrum[:8])
+        out_ref[c, 0, :8] = top[:, :LANES]
+        out_ref[c, 1, :8] = top[:, LANES:]
+
+
+def backward_kernel(spectrum_ref, filter_ref, outer_ref, twist_ref, inner_ref, edge_ref, out_ref):
+    parts, own, _, blocks, _ = filter_ref.shape
+    slots = parts * blocks
+    cos, sin = twist_ref[0], twist_ref[1]
+    row = lax.broadcasted_iota(jnp.int32, (slots, LANES), 0)
+    lane = lax.broadcasted_iota(jnp.int32, (slots, LANES), 1)
+    corner = jnp.logical_and(row == 0, lane == 0)
+    head = lax.broadcasted_iota(jnp.int32, (8, 2 * LANES), 0) == 0
+    columns = []
+    for c in range(own):
+        filt_re = jnp.concatenate([filter_ref[part, c, 0] for part in range(parts)], axis=0)
+        filt_im = jnp.concatenate([filter_ref[part, c, 1] for part in range(parts)], axis=0)
+        re, im = spectrum_ref[c, 0], spectrum_ref[c, 1]
+        low, high = re * filt_re, im * filt_im
+        out_re = jnp.where(corner, low, low - high)
+        out_im = jnp.where(corner, high, re * filt_im + im * filt_re)
+        pair = split_pair(jnp.concatenate([out_re, out_im], axis=1))
+        back = multiply(pair, (inner_ref[0], inner_ref[1]), ROWS_COLS)
+        edge = multiply((pair[0][:16], pair[1][:16]), (edge_ref[0], edge_ref[1]), ROWS_COLS)
+        top = jnp.where(head, edge[:8], back[:8])
+        back = jnp.concatenate([top, back[8:]], axis=0)
+        re, im = back[:, :LANES], back[:, LANES:]
+        columns.append(jnp.concatenate([re * cos - im * sin, im * cos + re * sin], axis=0))
+    turned = split_pair(jnp.concatenate(columns, axis=1))
+    result = multiply((outer_ref[0], outer_ref[1]), turned, ROWS_COLS)
+    for part in range(parts):
+        for c in range(own):
+            out_ref[part, c] = result[part * blocks : (part + 1) * blocks, c * LANES : (c + 1) * LANES]
+
+
+def finish_kernel(conv_ref, signal_ref, gate_ref, skip_ref, out_ref):
+    channels, length = signal_ref.shape
+    blocks = length // LANES
+    skip = skip_ref[...]
+    for block in range(blocks):
+        where = slice(block * LANES, (block + 1) * LANES)
+        conv = conv_ref[pl.ds(block, channels, stride=blocks), :]
+        out_ref[:, where] = gate_ref[:, where] * (conv + skip * signal_ref[:, where])
+
+
+def call(kernel, shape, *operands, scratch=(), smem=0):
+    specs = [pl.BlockSpec(memory_space=pltpu.SMEM)] * smem
+    specs += [pl.BlockSpec(memory_space=pltpu.VMEM)] * (len(operands) - smem)
+    return pl.pallas_call(
+        kernel,
+        out_shape=jax.ShapeDtypeStruct(shape, jnp.float32),
+        in_specs=specs,
+        out_specs=pl.BlockSpec(memory_space=pltpu.VMEM),
+        scratch_shapes=scratch,
+    )(*operands)
+
+
+def exchange(values):
+    return lax.all_to_all(values, "ctx", split_axis=0, concat_axis=0, tiled=True)
+
+
+def by_channel(signal, gate, skip, filter_spectrum):
+    parts = lax.axis_size("ctx")
+    channels, length = signal.shape
+    blocks, own = length // LANES, channels // parts
+    table = tables(parts, blocks)
+    device = lax.axis_index("ctx")[None]
+    spread = call(spread_kernel, (channels * blocks, LANES), signal)
+    columns = exchange(spread.reshape(parts, own, blocks, LANES))
+    folded = call(
+        fold_kernel,
+        (channels, 2, blocks, LANES),
+        device,
+        filter_spectrum,
+        scratch=[pltpu.VMEM((2, channels * blocks, LANES), jnp.float32)],
+        smem=1,
+    )
+    filt = exchange(folded.reshape(parts, own, 2, blocks, LANES))
+    spectrum = call(
+        forward_kernel,
+        (own, 2, parts * blocks, LANES),
+        columns,
+        table["outer"],
+        table["twist"],
+        table["inner"],
+        table["edge"],
+    )
+    rows = call(
+        backward_kernel,
+        (parts, own, blocks, LANES),
+        spectrum,
+        filt,
+        table["outer"],
+        table["twist"],
+        table["inner_back"],
+        table["edge_back"],
+    )
+    convolved = exchange(rows).reshape(channels * blocks, LANES)
+    return call(finish_kernel, signal.shape, convolved, signal, gate, skip[:, None])
 
 
 def contract(form, left, right):
@@ -55,7 +315,7 @@
     return tuple((part.reshape(lead_shape + (length,)) for part in values))
 
 
-def shards(signal, gate, skip, filter_spectrum):
+def by_frequency(signal, gate, skip, filter_spectrum):
     parts_count = lax.axis_size("ctx")
     freq_rows = 2 * parts_count
     channels, tok_local = signal.shape
@@ -100,6 +360,14 @@
     return gate * (convolved[0] + skip[:, None] * signal)
 
 
+def shards(signal, gate, skip, filter_spectrum):
+    parts = lax.axis_size("ctx")
+    channels, length = signal.shape
+    if channels % parts == 0 and 2 * length == LANES * LANES:
+        return by_channel(signal, gate, skip, filter_spectrum)
+    return by_frequency(signal, gate, skip, filter_spectrum)
+
+
 def solution(mesh):
     return jax.shard_map(
         shards,

time: 357 us -> 82.4 us (0.23); the launches traced: 351 us -> 81.9 us
  local copies, waits for them, and re-layouts: 133 us -> 2.5 us
  blocking collectives: 69.5 us -> 0 us
  other arithmetic: 52 us -> 0 us
  Pallas kernels: 0 us -> 28.1 us
  matrix products: 27.2 us -> 0 us
  waiting for transfers between devices: 57.2 us -> 36.7 us
    unnamed x16 -> x8, local copies, waits for them, and re-layouts: 73.3 us -> 1.83 us
    all_to_all x2 -> x0, blocking collectives: 69.5 us -> none  [the longest x1 51.9 us: shards(): lax.all_to_all(stacked, 'ctx', split_axis=3, concat_axis=0, tiled=True)]
    unnamed x1 -> x0, other arithmetic: 38.3 us -> none
    pallas_call x0 -> x5, Pallas kernels: none -> 28.1 us  [call(): pl.pallas_call(kernel, out_shape=jax.ShapeDtypeStruct(shape, jnp.float32)...]
    dot_general x20 -> x0, matrix products: 27.2 us -> none  [contract(): return jnp.einsum(form, left, right, precision=lax.Precision.HIGHEST)]
    all_to_all x6 -> x0, local copies, waits for them, and re-layouts: 26.4 us -> none  [the longest x3 18.9 us: shards(): lax.all_to_all(stacked, 'ctx', split_axis=3, concat_axis=0, tiled=True)]
    another operation x11 -> x0, local copies, waits for them, and re-layouts: 23 us -> none  [the longest x1 15.4 us: shards(): stacked = jnp.stack(turned, axis=1)]
    all_to_all x2 -> x3, waiting for transfers between devices: 57.2 us -> 36.7 us  [exchange(): lax.all_to_all(values, 'ctx', split_axis=0, concat_axis=0, tiled=True)]
  transfers between devices with their start and end apart: 2 -> 3, of which waited for: 2 -> 3; matrix products, arithmetic and copies ran while one was open for 2% -> 1% of each run, Pallas kernels for 0% -> 22%
where the time goes in v1:
time: 82.4 us; the launch traced here: 81.9 us
  waiting for transfers between devices  36.7 us (45%)
  Pallas kernels  28.1 us (34%)
  starting transfers between devices  14.6 us (18%)
  local copies, waits for them, and re-layouts  2.5 us (3%)
    all_to_all x3, waiting for transfers between devices, exchange(): lax.all_to_all(values, 'ctx', split_axis=0, concat_axis=0, tiled=True)  36.7 us
    pallas_call x5, Pallas kernels, call(): pl.pallas_call(kernel, out_shape=jax.ShapeDtypeStruct(shape, jnp.float32)...  28.1 us
    all_to_all x3, starting transfers between devices, exchange(): lax.all_to_all(values, 'ctx', split_axis=0, concat_axis=0, tiled=True)  14.6 us
    unnamed x8, local copies, waits for them, and re-layouts  1.83 us
  transfers between devices with their start and end apart: 3, of which 3 were waited for; matrix products, arithmetic and copies ran while one was open for 1% of the time, Pallas kernels for 22%

profile of v1, /device:TPU:0, one launch (start us, length us, event | category | flops | bytes accessed | tf_op | source)
XLA Modules:
  0.0 81.9 jit_solution(10937832463218469170)
XLA Ops:
  0.0 2.3 %shard_map.100 = f32[1024,128]{1,0:T(8,128)} custom-call(f32[16,8192]{1,0:T(8,128)} %signal_ref.3), custom_call_target="tpu_custom_call" | custom-call | tf_op jit(solution)/shard_map/pallas_call | solution.py:216
  2.3 7.3 %all-to-all-start = ((f32[8,2,64,128]{3,2,1,0:T(8,128)}), f32[8,2,64,128]{3,2,1,0:T(8,128)S(1)}, u32[]{:S(2)}, u32[]{:S(2)}) async-start(f32[8,2,64,128]{3,2,1,0:T(8,128)} %bitcast.6), calls=%async_computation | async-start | bytes 1048576 | tf_op jit(solution)/shard_map/all_to_all | solution.py:226
  9.6 12.2 %shard_map.102 = f32[16,2,64,128]{3,2,1,0:T(8,128)} custom-call(s32[1]{0:T(128)} %bitcast.1.device_ref, f32[2,2,16,8192]{3,2,1,0:T(8,128)} %filter_ref.1), custom_call_target="tpu_custom_call" | custom-call | tf_op jit(solution)/shard_map/pallas_call | solution.py:216
  21.8 2.3 %all-to-all-done.x_ref = f32[8,2,64,128]{3,2,1,0:T(8,128)S(1)} async-done(((f32[8,2,64,128]{3,2,1,0:T(8,128)}), f32[8,2,64,128]{3,2,1,0:T(8,128)S(1)}, u32[]{:S(2)}, u32[]{:S(2)}) %all-to-all-start) | async-done | bytes 524320 | tf_op jit(solution)/shard_map/all_to_all | solution.py:226
  24.0 0.0 copy-start.1
  24.0 3.6 %all-to-all-start.1 = ((f32[8,2,2,64,128]{4,3,2,1,0:T(8,128)}), f32[8,2,2,64,128]{4,3,2,1,0:T(8,128)S(1)}, u32[]{:S(2)}, u32[]{:S(2)}) async-start(f32[8,2,2,64,128]{4,3,2,1,0:T(8,128)} %bitcast.5), calls=%async_computation.1 | async-start | bytes 2097152 | tf_op jit(solution)/shard_map/all_to_all | solution.py:226
  27.7 0.0 copy-done.1
  27.7 5.5 %shard_map.101.spectrum_ref = f32[2,2,512,128]{3,2,1,0:T(8,128)} custom-call(f32[8,2,64,128]{3,2,1,0:T(8,128)} %copy-done.1, bf16[2,512,1024]{2,1,0:T(8,128)(2,1)} %constant.18.clone.outer_ref, f32[2,512,128]{2,1,0:T(8,128)} %constant.19.clone.twist_ref, bf16[2,256,256]{2,1,0:T(8,128)(2,1)} %constant.20.clone.inner_ref, ...), custom_call_target="tpu_custom_call" | custom-call | tf_op jit(solution)/shard_map/pallas_call | solution.py:216
  33.2 0.0 copy-start.3
  33.2 20.5 %all-to-all-done.1.filter_ref = f32[8,2,2,64,128]{4,3,2,1,0:T(8,128)S(1)} async-done(((f32[8,2,2,64,128]{4,3,2,1,0:T(8,128)}), f32[8,2,2,64,128]{4,3,2,1,0:T(8,128)S(1)}, u32[]{:S(2)}, u32[]{:S(2)}) %all-to-all-start.1) | async-done | bytes 1048608 | tf_op jit(solution)/shard_map/all_to_all | solution.py:226
  53.6 0.0 copy-start
  53.6 1.0 %copy-done = f32[8,2,2,64,128]{4,3,2,1,0:T(8,128)} copy-done((f32[8,2,2,64,128]{4,3,2,1,0:T(8,128)}, f32[8,2,2,64,128]{4,3,2,1,0:T(8,128)S(1)}, u32[]{:S(2)}) %copy-start) | copy-done | bytes 1048600
  54.7 5.7 %shard_map.103 = f32[8,2,64,128]{3,2,1,0:T(8,128)} custom-call(f32[2,2,512,128]{3,2,1,0:T(8,128)} %shard_map.101.spectrum_ref, f32[8,2,2,64,128]{4,3,2,1,0:T(8,128)} %copy-done, bf16[2,512,1024]{2,1,0:T(8,128)(2,1)} %constant.18.clone.outer_ref, f32[2,512,128]{2,1,0:T(8,128)} %constant.19.clone.twist_ref, bf16[2,256,256]{2,1,0:T(8,128)(2,1)} %constant.22.clone.inner_ref, ...), custom_call_target="tpu_custom_call" | custom-call | tf_op jit(solution)/shard_map/pallas_call | solution.py:216
  60.3 3.6 %all-to-all-start.2 = ((f32[8,2,64,128]{3,2,1,0:T(8,128)}), f32[8,2,64,128]{3,2,1,0:T(8,128)S(1)}, u32[]{:S(2)}, u32[]{:S(2)}) async-start(f32[8,2,64,128]{3,2,1,0:T(8,128)} %shard_map.103), calls=%async_computation.2 | async-start | bytes 1048576 | tf_op jit(solution)/shard_map/all_to_all | solution.py:226
  64.0 0.0 copy-done.3
  64.0 0.7 copy.11.skip_ref
  64.6 14.0 %all-to-all-done.2 = f32[8,2,64,128]{3,2,1,0:T(8,128)S(1)} async-done(((f32[8,2,64,128]{3,2,1,0:T(8,128)}), f32[8,2,64,128]{3,2,1,0:T(8,128)S(1)}, u32[]{:S(2)}, u32[]{:S(2)}) %all-to-all-start.2) | async-done | bytes 524320 | tf_op jit(solution)/shard_map/all_to_all | solution.py:226
  78.6 0.0 copy-start.2
  78.6 0.8 copy-done.2
  79.4 2.5 %shard_map.104 = f32[16,8192]{1,0:T(8,128)} custom-call(f32[1024,128]{1,0:T(8,128)} %bitcast.7, f32[16,8192]{1,0:T(8,128)} %signal_ref.3, f32[16,8192]{1,0:T(8,128)} %gate_ref.1, f32[16,1]{1,0:T(8,128)} %copy.11.skip_ref), custom_call_target="tpu_custom_call" | custom-call | tf_op jit(solution)/shard_map/pallas_call | solution.py:216
Async XLA Ops:
  2.3 21.8 %all-to-all-start = ((f32[8,2,64,128]{3,2,1,0:T(8,128)}), f32[8,2,64,128]{3,2,1,0:T(8,128)S(1)}, u32[]{:S(2)}, u32[]{:S(2)}) async-start(f32[8,2,64,128]{3,2,1,0:T(8,128)} %bitcast.6), calls=%async_computation | async-start | bytes 1048576 | tf_op jit(solution)/shard_map/all_to_all | solution.py:226
  24.0 3.6 %copy-start.1 = (f32[8,2,64,128]{3,2,1,0:T(8,128)}, f32[8,2,64,128]{3,2,1,0:T(8,128)S(1)}, u32[]{:S(2)}) copy-start(f32[8,2,64,128]{3,2,1,0:T(8,128)S(1)} %all-to-all-done.x_ref) | copy-start | bytes 1572868
  24.0 29.6 %all-to-all-start.1 = ((f32[8,2,2,64,128]{4,3,2,1,0:T(8,128)}), f32[8,2,2,64,128]{4,3,2,1,0:T(8,128)S(1)}, u32[]{:S(2)}, u32[]{:S(2)}) async-start(f32[8,2,2,64,128]{4,3,2,1,0:T(8,128)} %bitcast.5), calls=%async_computation.1 | async-start | bytes 2097152 | tf_op jit(solution)/shard_map/all_to_all | solution.py:226
  33.2 30.8 %copy-start.3 = (f32[16]{0:T(128)S(1)}, f32[16]{0:T(128)}, u32[]{:S(2)}) copy-start(f32[16]{0:T(128)} %param.12) | copy-start | bytes 196
  53.6 1.0 %copy-start = (f32[8,2,2,64,128]{4,3,2,1,0:T(8,128)}, f32[8,2,2,64,128]{4,3,2,1,0:T(8,128)S(1)}, u32[]{:S(2)}) copy-start(f32[8,2,2,64,128]{4,3,2,1,0:T(8,128)S(1)} %all-to-all-done.1.filter_ref) | copy-start | bytes 3145732
  60.3 18.3 %all-to-all-start.2 = ((f32[8,2,64,128]{3,2,1,0:T(8,128)}), f32[8,2,64,128]{3,2,1,0:T(8,128)S(1)}, u32[]{:S(2)}, u32[]{:S(2)}) async-start(f32[8,2,64,128]{3,2,1,0:T(8,128)} %shard_map.103), calls=%async_computation.2 | async-start | bytes 1048576 | tf_op jit(solution)/shard_map/all_to_all | solution.py:226
  78.6 0.8 copy-start.2
